TPU v7x, 512 devices: a whole 4x4x16 slice. The times are simulated.
512 devices in a mesh: row: 16 (over z), col: 16 (over x, y), layer: 2 (over core).
Axes of the slice: x: 4, y: 4, z: 16, core: 2. Of those that a mesh axis runs over, the one named last changes fastest.
Arguments:
- a_tiles: bfloat16 [16, 16, 2, 512, 512], P('row', 'col'), as said below
- a_where: int32 [16, 16, 2], P('row', 'col'), may hold values from 0 to 3, as said below
- a_count: int32 [16, 16], P('row', 'col'), may hold values from 1 to 2, as said below
- b_slab: bfloat16 [16, 16, 1024, 384], P('row', 'col'), may hold values from -6 to 6
Outputs:
- flow_next: float32 [16384, 6144], P(('row', 'layer'), 'col')
Inputs may be any that keep to these rules, and one draw needn't show every extreme that they name: `a_where`: the positions of the slots of one block are distinct. The live slots of a block are its first a_count ones; some block has all 2 slots live. `a_tiles`: entries of slots that are not live are ignored.
All inputs are finite; a program needn't handle non-finite values.
Results may differ from a plain program's by a relative error of at most 0.0003.
Values may be sent and summed in bfloat16 or wider, within the bound.
No kernel may reach another device: no remote copies, remote signals or barrier semaphores. Data moves between devices by JAX's collectives and lax.ppermute only.
A program may use at most 64 MiB of HBM per device.

v0:
```python
import jax
import jax.numpy as jnp
from jax import lax
from jax.sharding import PartitionSpec as P

SPAN = 2


def from_behind(value, axis, steps):
    count = lax.axis_size(axis)
    pairs = [(source, (source + steps) % count) for source in range(count)]
    return lax.ppermute(value, axis, pairs)


def tile_products(partial_sum, tile_data, tile_place, live_count, slab_block):
    tile_size = tile_data.shape[-1]
    slab_cols = slab_block.shape[-1]
    slab_rows = slab_block.reshape(SPAN, tile_size, slab_cols)
    tile_rows = jnp.arange(SPAN, dtype=jnp.int32)
    for slot_index in range(tile_data.shape[0]):
        position = tile_place[slot_index]
        source = lax.dynamic_index_in_dim(slab_rows, position % SPAN, 0, keepdims=False)
        product = jnp.dot(tile_data[slot_index], source, preferred_element_type=jnp.float32)
        live_mask = (slot_index < live_count).astype(jnp.float32)
        target = (tile_rows == position // SPAN).astype(jnp.float32) * live_mask
        partial_sum = partial_sum + target[:, None, None] * product[None]
    return partial_sum


def local(a_tiles, a_where, a_count, b_slab):
    tile_data = a_tiles[0, 0]
    tile_place = a_where[0, 0]
    live_count = a_count[0, 0]
    slab_block = b_slab[0, 0]
    layer_index = lax.axis_index("layer")
    grid_size = lax.axis_size("col")
    rounds = grid_size // lax.axis_size("layer")
    tile_size = tile_data.shape[-1]
    slab_cols = slab_block.shape[-1]
    partial_sum = jnp.zeros((SPAN, tile_size, slab_cols), jnp.float32)
    moved_tiles = from_behind((tile_data, tile_place, live_count), "col", -rounds)
    moved_slab = from_behind(slab_block, "row", -rounds)
    upper = layer_index == 1
    tile_data = jnp.where(upper, moved_tiles[0], tile_data)
    tile_place = jnp.where(upper, moved_tiles[1], tile_place)
    live_count = jnp.where(upper, moved_tiles[2], live_count)
    slab_block = jnp.where(upper, moved_slab, slab_block)
    for turn_index in range(rounds):
        partial_sum = tile_products(partial_sum, tile_data, tile_place, live_count, slab_block)
        if turn_index + 1 < rounds:
            tile_data, tile_place, live_count = from_behind(
                (tile_data, tile_place, live_count), "col", -1
            )
            slab_block = from_behind(slab_block, "row", -1)
    partial_block = partial_sum.reshape(SPAN * tile_size, slab_cols)
    matrix_order = grid_size * SPAN * tile_size
    shared = lax.psum_scatter(partial_block, "layer", scatter_dimension=0, tiled=True)
    inflated = shared * shared
    column_mass = lax.psum(jnp.sum(inflated, axis=0), ("row", "layer"))
    return inflated / (column_mass / matrix_order + 1e-06)


def solution(mesh):
    in_specs = (
        P("row", "col", None, None, None),
        P("row", "col", None),
        P("row", "col"),
        P("row", "col", None, None),
    )
    out_specs = P(("row", "layer"), "col")
    return jax.shard_map(local, mesh=mesh, in_specs=in_specs, out_specs=out_specs, check_vma=False)
```

profile of v0, /device:TPU:2, one launch (start us, length us, event | category | flops | bytes accessed | tf_op | source)
XLA Modules:
  0.0 409.8 jit_solution(3143512087581438021)
XLA Ops:
  6.5 4.0 collective-permute-start
  10.6 3.3 collective-permute-start.1
  13.9 15.7 %collective-permute-start.3 = (bf16[1024,384]{1,0:T(8,128)(2,1)}, bf16[1024,384]{1,0:T(8,128)(2,1)}, u32[]{:S(2)}, u32[]{:S(2)}) collective-permute-start(bf16[1024,384]{1,0:T(8,128)(2,1)} %bitcast.271), channel_id=1, source_target_pairs={{0,256},{32,288},{64,320},{96,352},{128,384},{160,416},{192,448},{... | collective-permute-start | bytes 2359304 | tf_op jit(solution)/shard_map/ppermute | solution.py:12
  29.6 4.0 collective-permute-start.2
  34.9 20.6 %collective-permute-start.5 = (s32[]{:T(128)}, s32[]{:T(128)}, u32[]{:S(2)}, u32[]{:S(2)}) collective-permute-start(s32[]{:T(128)} %select_n.195), channel_id=1, source_target_pairs={{0,30},{2,0},{4,2},{6,4},{8,6},{10,8},{12,10},{14,12},{16,14},{18,... | collective-permute-start | bytes 20 | tf_op jit(solution)/shard_map/ppermute | solution.py:12
  61.8 1.9 collective-permute-start.4
  65.1 1.9 collective-permute-start.9
  67.1 3.7 collective-permute-done.9
  71.9 4.0 collective-permute-start.13
  85.3 1.9 collective-permute-start.17
  87.2 3.7 collective-permute-done.17
  92.0 4.0 collective-permute-start.21
  105.5 3.6 collective-permute-start.12
  110.4 4.3 %collective-permute-start.25 = (s32[]{:T(128)}, s32[]{:T(128)}, u32[]{:S(2)}, u32[]{:S(2)}) collective-permute-start(s32[]{:T(128)} %collective-permute-done.21), channel_id=1, source_target_pairs={{0,30},{2,0},{4,2},{6,4},{8,6},{10,8},{12,10},{14,12},{16,14},{18,... | collective-permute-start | bytes 20 | tf_op jit(solution)/shard_map/ppermute | solution.py:12
  114.7 11.8 %collective-permute-done.25 = s32[]{:T(128)} collective-permute-done((s32[]{:T(128)}, s32[]{:T(128)}, u32[]{:S(2)}, u32[]{:S(2)}) %collective-permute-start.25) | collective-permute-done | bytes 36 | tf_op jit(solution)/shard_map/ppermute | solution.py:12
  127.5 4.3 %collective-permute-start.29 = (s32[]{:T(128)}, s32[]{:T(128)}, u32[]{:S(2)}, u32[]{:S(2)}) collective-permute-start(s32[]{:T(128)} %collective-permute-done.25), channel_id=1, source_target_pairs={{0,30},{2,0},{4,2},{6,4},{8,6},{10,8},{12,10},{14,12},{16,14},{18,... | collective-permute-start | bytes 20 | tf_op jit(solution)/shard_map/ppermute | solution.py:12
  137.6 1.9 collective-permute-start.10
  141.0 5.6 %collective-permute-start.16 = (s32[2]{0:T(128)S(1)}, s32[2]{0:T(128)S(1)}, u32[]{:S(2)}, u32[]{:S(2)}) collective-permute-start(s32[2]{0:T(128)S(1)} %collective-permute-done.12), channel_id=1, source_target_pairs={{0,30},{2,0},{4,2},{6,4},{8,6},{10,8},{12,10},{14,12},{16,14},{18,... | collective-permute-start | bytes 32 | tf_op jit(solution)/shard_map/ppermute | solution.py:12
  146.6 12.9 %collective-permute-done.16 = s32[2]{0:T(128)S(1)} collective-permute-done((s32[2]{0:T(128)S(1)}, s32[2]{0:T(128)S(1)}, u32[]{:S(2)}, u32[]{:S(2)}) %collective-permute-start.16) | collective-permute-done | bytes 40 | tf_op jit(solution)/shard_map/ppermute | solution.py:12
  166.3 3.8 collective-permute-start.7
  170.1 4.3 %collective-permute-start.14 = (bf16[2,512,512]{2,1,0:T(8,128)(2,1)}, bf16[2,512,512]{2,1,0:T(8,128)(2,1)}, u32[]{:S(2)}, u32[]{:S(2)}) collective-permute-start(bf16[2,512,512]{2,1,0:T(8,128)(2,1)} %collective-permute-done.10), channel_id=1, source_target_pairs={{0,30},{2,0},{4,2},{6,4},{8,6},{10,8},{12,10},{14,12},{16,14},{18,... | collective-permute-start | bytes 3145736 | tf_op jit(solution)/shard_map/ppermute | solution.py:12
  174.5 2.0 collective-permute-start.20
  176.5 15.9 %collective-permute-done.20 = s32[2]{0:T(128)S(1)} collective-permute-done((s32[2]{0:T(128)S(1)}, s32[2]{0:T(128)S(1)}, u32[]{:S(2)}, u32[]{:S(2)}) %collective-permute-start.20) | collective-permute-done | bytes 40 | tf_op jit(solution)/shard_map/ppermute | solution.py:12
  198.4 2.2 collective-permute-start.11
  200.7 6.5 %collective-permute-start.24 = (s32[2]{0:T(128)S(1)}, s32[2]{0:T(128)S(1)}, u32[]{:S(2)}, u32[]{:S(2)}) collective-permute-start(s32[2]{0:T(128)S(1)} %collective-permute-done.20), channel_id=1, source_target_pairs={{0,30},{2,0},{4,2},{6,4},{8,6},{10,8},{12,10},{14,12},{16,14},{18,... | collective-permute-start | bytes 32 | tf_op jit(solution)/shard_map/ppermute | solution.py:12
  214.5 6.3 %collective-permute-start.18 = (bf16[2,512,512]{2,1,0:T(8,128)(2,1)}, bf16[2,512,512]{2,1,0:T(8,128)(2,1)}, u32[]{:S(2)}, u32[]{:S(2)}) collective-permute-start(bf16[2,512,512]{2,1,0:T(8,128)(2,1)} %collective-permute-done.14), channel_id=1, source_target_pairs={{0,30},{2,0},{4,2},{6,4},{8,6},{10,8},{12,10},{14,12},{16,14},{18,... | collective-permute-start | bytes 3145736 | tf_op jit(solution)/shard_map/ppermute | solution.py:12
  220.8 2.0 collective-permute-start.15
  222.9 1.9 collective-permute-start.28
  224.9 11.7 %collective-permute-done.28 = s32[2]{0:T(128)S(1)} collective-permute-done((s32[2]{0:T(128)S(1)}, s32[2]{0:T(128)S(1)}, u32[]{:S(2)}, u32[]{:S(2)}) %collective-permute-start.28) | collective-permute-done | bytes 40 | tf_op jit(solution)/shard_map/ppermute | solution.py:12
  242.5 2.2 collective-permute-start.19
  244.7 6.5 %collective-permute-start.22 = (bf16[2,512,512]{2,1,0:T(8,128)(2,1)}, bf16[2,512,512]{2,1,0:T(8,128)(2,1)}, u32[]{:S(2)}, u32[]{:S(2)}) collective-permute-start(bf16[2,512,512]{2,1,0:T(8,128)(2,1)} %collective-permute-done.18), channel_id=1, source_target_pairs={{0,30},{2,0},{4,2},{6,4},{8,6},{10,8},{12,10},{14,12},{16,14},{18,... | collective-permute-start | bytes 3145736 | tf_op jit(solution)/shard_map/ppermute | solution.py:12
  252.2 8.7 %collective-permute-done.19 = bf16[1024,384]{1,0:T(8,128)(2,1)} collective-permute-done((bf16[1024,384]{1,0:T(8,128)(2,1)}, bf16[1024,384]{1,0:T(8,128)(2,1)}, u32[]{:S(2)}, u32[]{:S(2)}) %collective-permute-start.19) | collective-permute-done | bytes 786464 | tf_op jit(solution)/shard_map/ppermute | solution.py:12
  260.9 2.0 collective-permute-start.23
  265.8 2.2 collective-permute-done.22
  268.0 6.5 %collective-permute-start.26 = (bf16[2,512,512]{2,1,0:T(8,128)(2,1)}, bf16[2,512,512]{2,1,0:T(8,128)(2,1)S(1)}, u32[]{:S(2)}, u32[]{:S(2)}) collective-permute-start(bf16[2,512,512]{2,1,0:T(8,128)(2,1)} %collective-permute-done.22), channel_id=1, source_target_pairs={{0,30},{2,0},{4,2},{6,4},{8,6},{10,8},{12,10},{14,12},{16,14},{18,... | collective-permute-start | bytes 3145736 | tf_op jit(solution)/shard_map/ppermute | solution.py:12
  278.8 2.9 collective-permute-start.27
  284.9 2.5 fusion.21
  287.4 4.3 %collective-permute-done.26 = bf16[2,512,512]{2,1,0:T(8,128)(2,1)S(1)} collective-permute-done((bf16[2,512,512]{2,1,0:T(8,128)(2,1)}, bf16[2,512,512]{2,1,0:T(8,128)(2,1)S(1)}, u32[]{:S(2)}, u32[]{:S(2)}) %collective-permute-start.26) | collective-permute-done | bytes 1048608 | tf_op jit(solution)/shard_map/ppermute | solution.py:12
  291.7 6.4 %collective-permute-start.30 = (bf16[2,512,512]{2,1,0:T(8,128)(2,1)S(1)}, bf16[2,512,512]{2,1,0:T(8,128)(2,1)S(1)}, u32[]{:S(2)}, u32[]{:S(2)}) collective-permute-start(bf16[2,512,512]{2,1,0:T(8,128)(2,1)S(1)} %collective-permute-done.26), channel_id=1, source_target_pairs={{0,30},{2,0},{4,2},{6,4},{8,6},{10,8},{12,10},{14,12},{16,14},{18,... | collective-permute-start | bytes 3145736 | tf_op jit(solution)/shard_map/ppermute | solution.py:12
  298.0 2.5 fusion.22
  300.6 2.0 collective-permute-start.31
  302.6 2.4 fusion.19
  305.0 2.4 fusion.20
  310.0 4.5 %collective-permute-done.31 = bf16[1024,384]{1,0:T(8,128)(2,1)S(1)} collective-permute-done((bf16[1024,384]{1,0:T(8,128)(2,1)S(1)}, bf16[1024,384]{1,0:T(8,128)(2,1)S(1)}, u32[]{:S(2)}, u32[]{:S(2)}) %collective-permute-start.31) | collective-permute-done | bytes 786464 | tf_op jit(solution)/shard_map/ppermute | solution.py:12
  317.1 6.3 %fusion = f32[1024,384]{1,0:T(8,128)} fusion(f32[512,384]{1,0:T(8,128)} %fusion.15, f32[1024]{0:T(1024)S(1)} %bitcast.292, f32[512,384]{1,0:T(8,128)} %fusion.16, f32[1024]{0:T(1024)S(1)} %bitcast.293, f32[512,384]{1,0:T(8,128)} %fusion.17, f32[1024]{0:T(1024)S(1)} %bitcast.290, f32[512,384]{1,0:T(8,128)} %fusion.18, f32[1024]{0:T(1024)S(1)} %bitcast.291, ...), kind=kLoop, calls=%fused_computation.1 | loop fusion | flops 12189696 | bytes 14221312 | tf_op jit(solution)/shard_map/add | solution.py:26
  323.4 26.6 %reduce-scatter.2.cloned.1.call-done = f32[512,384]{1,0:T(8,128)} async-done(((f32[1024,384]{1,0:T(8,128)}), f32[512,384]{1,0:T(8,128)}) %reduce-scatter.2.cloned.1.call-update) | async-done | bytes 786448 | tf_op jit(solution)/shard_map/reduce_scatter | solution.py:57
  351.3 49.6 %psum.7 = f32[384]{0:T(512)S(1)} all-reduce(f32[384]{0:T(512)S(1)} %multiply_reduce_fusion), channel_id=1, replica_groups=mesh['row'=16,'col'=16,'layer'=2] {'row','layer'}, use_global_device_ids=true, to_apply=%region_2.3 | all-reduce | flops 384 | bytes 3072 | tf_op jit(solution)/shard_map/psum | solution.py:59
  400.9 2.1 multiply_divide_fusion
  (99 shorter events, 32.4 us)
Async XLA Ops:
  6.5 343.5 %reduce-scatter.2.cloned.1.call-start = ((), (), s32[]{:S(2)}) async-start(), calls=%async_computation.1 | async-start | bytes 2359296 | tf_op jit(solution)/shard_map/reduce_scatter | solution.py:57
  6.5 49.0 %collective-permute-start = (s32[2]{0:T(128)}, s32[2]{0:T(128)S(1)}, u32[]{:S(2)}, u32[]{:S(2)}) collective-permute-start(s32[2]{0:T(128)} %bitcast.294), channel_id=1, source_target_pairs={{0,16},{2,18},{4,20},{6,22},{8,24},{10,26},{12,28},{14,30},{16,0},... | collective-permute-start | bytes 32 | tf_op jit(solution)/shard_map/ppermute | solution.py:12
  10.6 23.7 %collective-permute-start.1 = (s32[]{:T(128)}, s32[]{:T(128)}, u32[]{:S(2)}, u32[]{:S(2)}) collective-permute-start(s32[]{:T(128)} %bitcast.2), channel_id=1, source_target_pairs={{0,16},{2,18},{4,20},{6,22},{8,24},{10,26},{12,28},{14,30},{16,0},... | collective-permute-start | bytes 20 | tf_op jit(solution)/shard_map/ppermute | solution.py:12
  13.9 151.1 %collective-permute-start.3 = (bf16[1024,384]{1,0:T(8,128)(2,1)}, bf16[1024,384]{1,0:T(8,128)(2,1)}, u32[]{:S(2)}, u32[]{:S(2)}) collective-permute-start(bf16[1024,384]{1,0:T(8,128)(2,1)} %bitcast.271), channel_id=1, source_target_pairs={{0,256},{32,288},{64,320},{96,352},{128,384},{160,416},{192,448},{... | collective-permute-start | bytes 2359304 | tf_op jit(solution)/shard_map/ppermute | solution.py:12
  29.6 72.4 %collective-permute-start.2 = (bf16[2,512,512]{2,1,0:T(8,128)(2,1)}, bf16[2,512,512]{2,1,0:T(8,128)(2,1)S(1)}, u32[]{:S(2)}, u32[]{:S(2)}) collective-permute-start(bf16[2,512,512]{2,1,0:T(8,128)(2,1)} %bitcast.270), channel_id=1, source_target_pairs={{0,16},{2,18},{4,20},{6,22},{8,24},{10,26},{12,28},{14,30},{16,0},... | collective-permute-start | bytes 3145736 | tf_op jit(solution)/shard_map/ppermute | solution.py:12
  34.9 29.0 %collective-permute-start.5 = (s32[]{:T(128)}, s32[]{:T(128)}, u32[]{:S(2)}, u32[]{:S(2)}) collective-permute-start(s32[]{:T(128)} %select_n.195), channel_id=1, source_target_pairs={{0,30},{2,0},{4,2},{6,4},{8,6},{10,8},{12,10},{14,12},{16,14},{18,... | collective-permute-start | bytes 20 | tf_op jit(solution)/shard_map/ppermute | solution.py:12
  61.8 14.2 %collective-permute-start.4 = (s32[2]{0:T(128)S(1)}, s32[2]{0:T(128)S(1)}, u32[]{:S(2)}, u32[]{:S(2)}) collective-permute-start(s32[2]{0:T(128)S(1)} %broadcast_select_fusion.2), channel_id=1, source_target_pairs={{0,30},{2,0},{4,2},{6,4},{8,6},{10,8},{12,10},{14,12},{16,14},{18,... | collective-permute-start | bytes 32 | tf_op jit(solution)/shard_map/ppermute | solution.py:12
  65.1 5.6 %collective-permute-start.9 = (s32[]{:T(128)}, s32[]{:T(128)}, u32[]{:S(2)}, u32[]{:S(2)}) collective-permute-start(s32[]{:T(128)} %collective-permute-done.5), channel_id=1, source_target_pairs={{0,30},{2,0},{4,2},{6,4},{8,6},{10,8},{12,10},{14,12},{16,14},{18,... | collective-permute-start | bytes 20 | tf_op jit(solution)/shard_map/ppermute | solution.py:12
  71.9 10.2 %collective-permute-start.13 = (s32[]{:T(128)}, s32[]{:T(128)}, u32[]{:S(2)}, u32[]{:S(2)}) collective-permute-start(s32[]{:T(128)} %collective-permute-done.9), channel_id=1, source_target_pairs={{0,30},{2,0},{4,2},{6,4},{8,6},{10,8},{12,10},{14,12},{16,14},{18,... | collective-permute-start | bytes 20 | tf_op jit(solution)/shard_map/ppermute | solution.py:12
  83.3 12.7 %collective-permute-start.8 = (s32[2]{0:T(128)S(1)}, s32[2]{0:T(128)S(1)}, u32[]{:S(2)}, u32[]{:S(2)}) collective-permute-start(s32[2]{0:T(128)S(1)} %collective-permute-done.4), channel_id=1, source_target_pairs={{0,30},{2,0},{4,2},{6,4},{8,6},{10,8},{12,10},{14,12},{16,14},{18,... | collective-permute-start | bytes 32 | tf_op jit(solution)/shard_map/ppermute | solution.py:12
  85.3 5.6 %collective-permute-start.17 = (s32[]{:T(128)}, s32[]{:T(128)}, u32[]{:S(2)}, u32[]{:S(2)}) collective-permute-start(s32[]{:T(128)} %collective-permute-done.13), channel_id=1, source_target_pairs={{0,30},{2,0},{4,2},{6,4},{8,6},{10,8},{12,10},{14,12},{16,14},{18,... | collective-permute-start | bytes 20 | tf_op jit(solution)/shard_map/ppermute | solution.py:12
  92.0 17.1 %collective-permute-start.21 = (s32[]{:T(128)}, s32[]{:T(128)}, u32[]{:S(2)}, u32[]{:S(2)}) collective-permute-start(s32[]{:T(128)} %collective-permute-done.17), channel_id=1, source_target_pairs={{0,30},{2,0},{4,2},{6,4},{8,6},{10,8},{12,10},{14,12},{16,14},{18,... | collective-permute-start | bytes 20 | tf_op jit(solution)/shard_map/ppermute | solution.py:12
  103.4 34.2 %collective-permute-start.6 = (bf16[2,512,512]{2,1,0:T(8,128)(2,1)S(1)}, bf16[2,512,512]{2,1,0:T(8,128)(2,1)S(1)}, u32[]{:S(2)}, u32[]{:S(2)}) collective-permute-start(bf16[2,512,512]{2,1,0:T(8,128)(2,1)S(1)} %broadcast_select_fusion), channel_id=1, source_target_pairs={{0,30},{2,0},{4,2},{6,4},{8,6},{10,8},{12,10},{14,12},{16,14},{18,... | collective-permute-start | bytes 3145736 | tf_op jit(solution)/shard_map/ppermute | solution.py:12
  105.5 26.4 %collective-permute-start.12 = (s32[2]{0:T(128)S(1)}, s32[2]{0:T(128)S(1)}, u32[]{:S(2)}, u32[]{:S(2)}) collective-permute-start(s32[2]{0:T(128)S(1)} %collective-permute-done.8), channel_id=1, source_target_pairs={{0,30},{2,0},{4,2},{6,4},{8,6},{10,8},{12,10},{14,12},{16,14},{18,... | collective-permute-start | bytes 32 | tf_op jit(solution)/shard_map/ppermute | solution.py:12
  110.4 16.1 %collective-permute-start.25 = (s32[]{:T(128)}, s32[]{:T(128)}, u32[]{:S(2)}, u32[]{:S(2)}) collective-permute-start(s32[]{:T(128)} %collective-permute-done.21), channel_id=1, source_target_pairs={{0,30},{2,0},{4,2},{6,4},{8,6},{10,8},{12,10},{14,12},{16,14},{18,... | collective-permute-start | bytes 20 | tf_op jit(solution)/shard_map/ppermute | solution.py:12
  127.5 12.1 %collective-permute-start.29 = (s32[]{:T(128)}, s32[]{:T(128)}, u32[]{:S(2)}, u32[]{:S(2)}) collective-permute-start(s32[]{:T(128)} %collective-permute-done.25), channel_id=1, source_target_pairs={{0,30},{2,0},{4,2},{6,4},{8,6},{10,8},{12,10},{14,12},{16,14},{18,... | collective-permute-start | bytes 20 | tf_op jit(solution)/shard_map/ppermute | solution.py:12
  137.6 32.4 %collective-permute-start.10 = (bf16[2,512,512]{2,1,0:T(8,128)(2,1)S(1)}, bf16[2,512,512]{2,1,0:T(8,128)(2,1)}, u32[]{:S(2)}, u32[]{:S(2)}) collective-permute-start(bf16[2,512,512]{2,1,0:T(8,128)(2,1)S(1)} %collective-permute-done.6), channel_id=1, source_target_pairs={{0,30},{2,0},{4,2},{6,4},{8,6},{10,8},{12,10},{14,12},{16,14},{18,... | collective-permute-start | bytes 3145736 | tf_op jit(solution)/shard_map/ppermute | solution.py:12
  141.0 18.5 %collective-permute-start.16 = (s32[2]{0:T(128)S(1)}, s32[2]{0:T(128)S(1)}, u32[]{:S(2)}, u32[]{:S(2)}) collective-permute-start(s32[2]{0:T(128)S(1)} %collective-permute-done.12), channel_id=1, source_target_pairs={{0,30},{2,0},{4,2},{6,4},{8,6},{10,8},{12,10},{14,12},{16,14},{18,... | collective-permute-start | bytes 32 | tf_op jit(solution)/shard_map/ppermute | solution.py:12
  166.3 32.2 %collective-permute-start.7 = (bf16[1024,384]{1,0:T(8,128)(2,1)S(1)}, bf16[1024,384]{1,0:T(8,128)(2,1)}, u32[]{:S(2)}, u32[]{:S(2)}) collective-permute-start(bf16[1024,384]{1,0:T(8,128)(2,1)S(1)} %broadcast_select_fusion.1), channel_id=1, source_target_pairs={{0,480},{32,0},{64,32},{96,64},{128,96},{160,128},{192,160},{224,1... | collective-permute-start | bytes 2359304 | tf_op jit(solution)/shard_map/ppermute | solution.py:12
  170.1 44.3 %collective-permute-start.14 = (bf16[2,512,512]{2,1,0:T(8,128)(2,1)}, bf16[2,512,512]{2,1,0:T(8,128)(2,1)}, u32[]{:S(2)}, u32[]{:S(2)}) collective-permute-start(bf16[2,512,512]{2,1,0:T(8,128)(2,1)} %collective-permute-done.10), channel_id=1, source_target_pairs={{0,30},{2,0},{4,2},{6,4},{8,6},{10,8},{12,10},{14,12},{16,14},{18,... | collective-permute-start | bytes 3145736 | tf_op jit(solution)/shard_map/ppermute | solution.py:12
  174.5 17.9 %collective-permute-start.20 = (s32[2]{0:T(128)S(1)}, s32[2]{0:T(128)S(1)}, u32[]{:S(2)}, u32[]{:S(2)}) collective-permute-start(s32[2]{0:T(128)S(1)} %collective-permute-done.16), channel_id=1, source_target_pairs={{0,30},{2,0},{4,2},{6,4},{8,6},{10,8},{12,10},{14,12},{16,14},{18,... | collective-permute-start | bytes 32 | tf_op jit(solution)/shard_map/ppermute | solution.py:12
  198.4 22.4 %collective-permute-start.11 = (bf16[1024,384]{1,0:T(8,128)(2,1)}, bf16[1024,384]{1,0:T(8,128)(2,1)}, u32[]{:S(2)}, u32[]{:S(2)}) collective-permute-start(bf16[1024,384]{1,0:T(8,128)(2,1)} %collective-permute-done.7), channel_id=1, source_target_pairs={{0,480},{32,0},{64,32},{96,64},{128,96},{160,128},{192,160},{224,1... | collective-permute-start | bytes 2359304 | tf_op jit(solution)/shard_map/ppermute | solution.py:12
  200.7 7.8 %collective-permute-start.24 = (s32[2]{0:T(128)S(1)}, s32[2]{0:T(128)S(1)}, u32[]{:S(2)}, u32[]{:S(2)}) collective-permute-start(s32[2]{0:T(128)S(1)} %collective-permute-done.20), channel_id=1, source_target_pairs={{0,30},{2,0},{4,2},{6,4},{8,6},{10,8},{12,10},{14,12},{16,14},{18,... | collective-permute-start | bytes 32 | tf_op jit(solution)/shard_map/ppermute | solution.py:12
  214.5 30.2 %collective-permute-start.18 = (bf16[2,512,512]{2,1,0:T(8,128)(2,1)}, bf16[2,512,512]{2,1,0:T(8,128)(2,1)}, u32[]{:S(2)}, u32[]{:S(2)}) collective-permute-start(bf16[2,512,512]{2,1,0:T(8,128)(2,1)} %collective-permute-done.14), channel_id=1, source_target_pairs={{0,30},{2,0},{4,2},{6,4},{8,6},{10,8},{12,10},{14,12},{16,14},{18,... | collective-permute-start | bytes 3145736 | tf_op jit(solution)/shard_map/ppermute | solution.py:12
  220.8 21.6 %collective-permute-start.15 = (bf16[1024,384]{1,0:T(8,128)(2,1)}, bf16[1024,384]{1,0:T(8,128)(2,1)}, u32[]{:S(2)}, u32[]{:S(2)}) collective-permute-start(bf16[1024,384]{1,0:T(8,128)(2,1)} %collective-permute-done.11), channel_id=1, source_target_pairs={{0,480},{32,0},{64,32},{96,64},{128,96},{160,128},{192,160},{224,1... | collective-permute-start | bytes 2359304 | tf_op jit(solution)/shard_map/ppermute | solution.py:12
  222.9 13.7 %collective-permute-start.28 = (s32[2]{0:T(128)S(1)}, s32[2]{0:T(128)S(1)}, u32[]{:S(2)}, u32[]{:S(2)}) collective-permute-start(s32[2]{0:T(128)S(1)} %collective-permute-done.24), channel_id=1, source_target_pairs={{0,30},{2,0},{4,2},{6,4},{8,6},{10,8},{12,10},{14,12},{16,14},{18,... | collective-permute-start | bytes 32 | tf_op jit(solution)/shard_map/ppermute | solution.py:12
  242.5 18.4 %collective-permute-start.19 = (bf16[1024,384]{1,0:T(8,128)(2,1)}, bf16[1024,384]{1,0:T(8,128)(2,1)}, u32[]{:S(2)}, u32[]{:S(2)}) collective-permute-start(bf16[1024,384]{1,0:T(8,128)(2,1)} %collective-permute-done.15), channel_id=1, source_target_pairs={{0,480},{32,0},{64,32},{96,64},{128,96},{160,128},{192,160},{224,1... | collective-permute-start | bytes 2359304 | tf_op jit(solution)/shard_map/ppermute | solution.py:12
  244.7 23.3 %collective-permute-start.22 = (bf16[2,512,512]{2,1,0:T(8,128)(2,1)}, bf16[2,512,512]{2,1,0:T(8,128)(2,1)}, u32[]{:S(2)}, u32[]{:S(2)}) collective-permute-start(bf16[2,512,512]{2,1,0:T(8,128)(2,1)} %collective-permute-done.18), channel_id=1, source_target_pairs={{0,30},{2,0},{4,2},{6,4},{8,6},{10,8},{12,10},{14,12},{16,14},{18,... | collective-permute-start | bytes 3145736 | tf_op jit(solution)/shard_map/ppermute | solution.py:12
  260.9 17.9 %collective-permute-start.23 = (bf16[1024,384]{1,0:T(8,128)(2,1)}, bf16[1024,384]{1,0:T(8,128)(2,1)S(1)}, u32[]{:S(2)}, u32[]{:S(2)}) collective-permute-start(bf16[1024,384]{1,0:T(8,128)(2,1)} %collective-permute-done.19), channel_id=1, source_target_pairs={{0,480},{32,0},{64,32},{96,64},{128,96},{160,128},{192,160},{224,1... | collective-permute-start | bytes 2359304 | tf_op jit(solution)/shard_map/ppermute | solution.py:12
  268.0 23.6 %collective-permute-start.26 = (bf16[2,512,512]{2,1,0:T(8,128)(2,1)}, bf16[2,512,512]{2,1,0:T(8,128)(2,1)S(1)}, u32[]{:S(2)}, u32[]{:S(2)}) collective-permute-start(bf16[2,512,512]{2,1,0:T(8,128)(2,1)} %collective-permute-done.22), channel_id=1, source_target_pairs={{0,30},{2,0},{4,2},{6,4},{8,6},{10,8},{12,10},{14,12},{16,14},{18,... | collective-permute-start | bytes 3145736 | tf_op jit(solution)/shard_map/ppermute | solution.py:12
  278.8 21.8 %collective-permute-start.27 = (bf16[1024,384]{1,0:T(8,128)(2,1)S(1)}, bf16[1024,384]{1,0:T(8,128)(2,1)S(1)}, u32[]{:S(2)}, u32[]{:S(2)}) collective-permute-start(bf16[1024,384]{1,0:T(8,128)(2,1)S(1)} %collective-permute-done.23), channel_id=1, source_target_pairs={{0,480},{32,0},{64,32},{96,64},{128,96},{160,128},{192,160},{224,1... | collective-permute-start | bytes 2359304 | tf_op jit(solution)/shard_map/ppermute | solution.py:12
  291.7 22.8 %collective-permute-start.30 = (bf16[2,512,512]{2,1,0:T(8,128)(2,1)S(1)}, bf16[2,512,512]{2,1,0:T(8,128)(2,1)S(1)}, u32[]{:S(2)}, u32[]{:S(2)}) collective-permute-start(bf16[2,512,512]{2,1,0:T(8,128)(2,1)S(1)} %collective-permute-done.26), channel_id=1, source_target_pairs={{0,30},{2,0},{4,2},{6,4},{8,6},{10,8},{12,10},{14,12},{16,14},{18,... | collective-permute-start | bytes 3145736 | tf_op jit(solution)/shard_map/ppermute | solution.py:12
  300.6 13.9 %collective-permute-start.31 = (bf16[1024,384]{1,0:T(8,128)(2,1)S(1)}, bf16[1024,384]{1,0:T(8,128)(2,1)S(1)}, u32[]{:S(2)}, u32[]{:S(2)}) collective-permute-start(bf16[1024,384]{1,0:T(8,128)(2,1)S(1)} %collective-permute-done.27), channel_id=1, source_target_pairs={{0,480},{32,0},{64,32},{96,64},{128,96},{160,128},{192,160},{224,1... | collective-permute-start | bytes 2359304 | tf_op jit(solution)/shard_map/ppermute | solution.py:12
Sparse Core Ops, SparseCore 0:
  323.6 26.4 reduce-scatter.1
where the time goes:
time: 412 us; the launch traced here: 410 us
  starting transfers between devices  142 us (34%)
  waiting for transfers between devices  108 us (26%)
  between operations  64.9 us (16%)
  blocking collectives  49.6 us (12%)
  matrix products  25.2 us (6%)
  other arithmetic  12.9 us (3%)
  local copies, waits for them, and re-layouts  6.23 us (2%)
    ppermute x32, starting transfers between devices, from_behind(): return lax.ppermute(value, axis, pairs)  142 us
    ppermute x32, waiting for transfers between devices, from_behind(): return lax.ppermute(value, axis, pairs)  81.8 us
    psum x1, blocking collectives, local(): column_mass = lax.psum(jnp.sum(inflated, axis=0), ('row', 'layer'))  49.6 us
    reduce_scatter x1, waiting for transfers between devices, local(): lax.psum_scatter(partial_block, 'layer', scatter_dimension=0, tiled=True)  26.6 us
    dot_general x16, matrix products, tile_products(): jnp.dot(tile_data[slot_index], source, preferred_element_type=jnp.float32)  25.2 us
  transfers between devices with their start and end apart: 33, of which 13 were waited for; matrix products, arithmetic and copies ran while one was open for 8% of the time, Pallas kernels for 0%

commit v1 on v0

--- a/solution.py
+++ b/solution.py
@@ -56,7 +56,9 @@
     matrix_order = grid_size * SPAN * tile_size
     shared = lax.psum_scatter(partial_block, "layer", scatter_dimension=0, tiled=True)
     inflated = shared * shared
-    column_mass = lax.psum(jnp.sum(inflated, axis=0), ("row", "layer"))
+    column_mass = jnp.sum(inflated, axis=0)
+    for b in ("row", "layer"):
+        column_mass = jax.lax.psum(column_mass, axis_name=b)
     return inflated / (column_mass / matrix_order + 1e-06)
 
 

time: 412 us -> 397 us (0.964)
  the two profiles are of different devices: /device:TPU:2 before, /device:TPU:1 now
where the time goes in v1:
time: 397 us; the launch traced here: 395 us
  starting transfers between devices  147 us (37%)
  waiting for transfers between devices  106 us (27%)
  between operations  64.7 us (16%)
  blocking collectives  32.9 us (8%)
  matrix products  25.2 us (6%)
  other arithmetic  13.2 us (3%)
  local copies, waits for them, and re-layouts  6.16 us (2%)
    ppermute x32, starting transfers between devices, from_behind(): return lax.ppermute(value, axis, pairs)  147 us
    ppermute x32, waiting for transfers between devices, from_behind(): return lax.ppermute(value, axis, pairs)  72.4 us
    reduce_scatter x1, waiting for transfers between devices, local(): lax.psum_scatter(partial_block, 'layer', scatter_dimension=0, tiled=True)  33.2 us
    psum x2, blocking collectives, local(): column_mass = jax.lax.psum(column_mass, axis_name=b)  32.9 us
    dot_general x16, matrix products, tile_products(): jnp.dot(tile_data[slot_index], source, preferred_element_type=jnp.float32)  25.2 us
  transfers between devices with their start and end apart: 33, of which 12 were waited for; matrix products, arithmetic and copies ran while one was open for 8% of the time, Pallas kernels for 0%

profile of v1, /device:TPU:1, one launch (start us, length us, event | category | flops | bytes accessed | tf_op | source)
XLA Modules:
  0.0 394.7 jit_solution(12059202971121806141)
XLA Ops:
  6.5 5.5 %collective-permute-start = (s32[2]{0:T(128)}, s32[2]{0:T(128)S(1)}, u32[]{:S(2)}, u32[]{:S(2)}) collective-permute-start(s32[2]{0:T(128)} %bitcast.294), channel_id=1, source_target_pairs={{0,16},{2,18},{4,20},{6,22},{8,24},{10,26},{12,28},{14,30},{16,0},... | collective-permute-start | bytes 32 | tf_op jit(solution)/shard_map/ppermute | solution.py:12
  12.0 1.9 collective-permute-start.1
  13.9 15.7 %collective-permute-start.3 = (bf16[1024,384]{1,0:T(8,128)(2,1)}, bf16[1024,384]{1,0:T(8,128)(2,1)}, u32[]{:S(2)}, u32[]{:S(2)}) collective-permute-start(bf16[1024,384]{1,0:T(8,128)(2,1)} %bitcast.271), channel_id=1, source_target_pairs={{0,256},{32,288},{64,320},{96,352},{128,384},{160,416},{192,448},{... | collective-permute-start | bytes 2359304 | tf_op jit(solution)/shard_map/ppermute | solution.py:12
  29.6 4.7 %collective-permute-start.2 = (bf16[2,512,512]{2,1,0:T(8,128)(2,1)}, bf16[2,512,512]{2,1,0:T(8,128)(2,1)S(1)}, u32[]{:S(2)}, u32[]{:S(2)}) collective-permute-start(bf16[2,512,512]{2,1,0:T(8,128)(2,1)} %bitcast.270), channel_id=1, source_target_pairs={{0,16},{2,18},{4,20},{6,22},{8,24},{10,26},{12,28},{14,30},{16,0},... | collective-permute-start | bytes 3145736 | tf_op jit(solution)/shard_map/ppermute | solution.py:12
  35.6 5.9 %collective-permute-start.5 = (s32[]{:T(128)}, s32[]{:T(128)}, u32[]{:S(2)}, u32[]{:S(2)}) collective-permute-start(s32[]{:T(128)} %select_n.195), channel_id=1, source_target_pairs={{0,30},{2,0},{4,2},{6,4},{8,6},{10,8},{12,10},{14,12},{16,14},{18,... | collective-permute-start | bytes 20 | tf_op jit(solution)/shard_map/ppermute | solution.py:12
  47.7 2.4 collective-permute-start.4
  51.7 2.1 collective-permute-start.9
  53.7 2.8 collective-permute-done.9
  57.7 5.4 %collective-permute-start.13 = (s32[]{:T(128)}, s32[]{:T(128)}, u32[]{:S(2)}, u32[]{:S(2)}) collective-permute-start(s32[]{:T(128)} %collective-permute-done.9), channel_id=1, source_target_pairs={{0,30},{2,0},{4,2},{6,4},{8,6},{10,8},{12,10},{14,12},{16,14},{18,... | collective-permute-start | bytes 20 | tf_op jit(solution)/shard_map/ppermute | solution.py:12
  70.6 14.0 %collective-permute-start.8 = (s32[2]{0:T(128)S(1)}, s32[2]{0:T(128)S(1)}, u32[]{:S(2)}, u32[]{:S(2)}) collective-permute-start(s32[2]{0:T(128)S(1)} %collective-permute-done.4), channel_id=1, source_target_pairs={{0,30},{2,0},{4,2},{6,4},{8,6},{10,8},{12,10},{14,12},{16,14},{18,... | collective-permute-start | bytes 32 | tf_op jit(solution)/shard_map/ppermute | solution.py:12
  84.6 3.6 collective-permute-start.17
  90.2 6.9 %collective-permute-start.21 = (s32[]{:T(128)}, s32[]{:T(128)}, u32[]{:S(2)}, u32[]{:S(2)}) collective-permute-start(s32[]{:T(128)} %collective-permute-done.17), channel_id=1, source_target_pairs={{0,30},{2,0},{4,2},{6,4},{8,6},{10,8},{12,10},{14,12},{16,14},{18,... | collective-permute-start | bytes 20 | tf_op jit(solution)/shard_map/ppermute | solution.py:12
  104.3 1.9 collective-permute-start.6
  109.7 1.9 collective-permute-start.25
  111.6 13.5 %collective-permute-done.25 = s32[]{:T(128)} collective-permute-done((s32[]{:T(128)}, s32[]{:T(128)}, u32[]{:S(2)}, u32[]{:S(2)}) %collective-permute-start.25) | collective-permute-done | bytes 36 | tf_op jit(solution)/shard_map/ppermute | solution.py:12
  126.2 5.5 %collective-permute-start.29 = (s32[]{:T(128)}, s32[]{:T(128)}, u32[]{:S(2)}, u32[]{:S(2)}) collective-permute-start(s32[]{:T(128)} %collective-permute-done.25), channel_id=1, source_target_pairs={{0,30},{2,0},{4,2},{6,4},{8,6},{10,8},{12,10},{14,12},{16,14},{18,... | collective-permute-start | bytes 20 | tf_op jit(solution)/shard_map/ppermute | solution.py:12
  137.9 1.9 collective-permute-start.10
  141.2 1.9 collective-permute-start.16
  143.2 14.7 %collective-permute-done.16 = s32[2]{0:T(128)S(1)} collective-permute-done((s32[2]{0:T(128)S(1)}, s32[2]{0:T(128)S(1)}, u32[]{:S(2)}, u32[]{:S(2)}) %collective-permute-start.16) | collective-permute-done | bytes 40 | tf_op jit(solution)/shard_map/ppermute | solution.py:12
  164.8 4.4 %collective-permute-start.7 = (bf16[1024,384]{1,0:T(8,128)(2,1)S(1)}, bf16[1024,384]{1,0:T(8,128)(2,1)}, u32[]{:S(2)}, u32[]{:S(2)}) collective-permute-start(bf16[1024,384]{1,0:T(8,128)(2,1)S(1)} %broadcast_select_fusion.1), channel_id=1, source_target_pairs={{0,480},{32,0},{64,32},{96,64},{128,96},{160,128},{192,160},{224,1... | collective-permute-start | bytes 2359304 | tf_op jit(solution)/shard_map/ppermute | solution.py:12
  169.3 5.5 %collective-permute-start.14 = (bf16[2,512,512]{2,1,0:T(8,128)(2,1)}, bf16[2,512,512]{2,1,0:T(8,128)(2,1)}, u32[]{:S(2)}, u32[]{:S(2)}) collective-permute-start(bf16[2,512,512]{2,1,0:T(8,128)(2,1)} %collective-permute-done.10), channel_id=1, source_target_pairs={{0,30},{2,0},{4,2},{6,4},{8,6},{10,8},{12,10},{14,12},{16,14},{18,... | collective-permute-start | bytes 3145736 | tf_op jit(solution)/shard_map/ppermute | solution.py:12
  174.9 1.9 collective-permute-start.20
  176.8 14.2 %collective-permute-done.20 = s32[2]{0:T(128)S(1)} collective-permute-done((s32[2]{0:T(128)S(1)}, s32[2]{0:T(128)S(1)}, u32[]{:S(2)}, u32[]{:S(2)}) %collective-permute-start.20) | collective-permute-done | bytes 40 | tf_op jit(solution)/shard_map/ppermute | solution.py:12
  196.8 2.1 collective-permute-start.11
  199.0 7.4 %collective-permute-start.24 = (s32[2]{0:T(128)S(1)}, s32[2]{0:T(128)S(1)}, u32[]{:S(2)}, u32[]{:S(2)}) collective-permute-start(s32[2]{0:T(128)S(1)} %collective-permute-done.20), channel_id=1, source_target_pairs={{0,30},{2,0},{4,2},{6,4},{8,6},{10,8},{12,10},{14,12},{16,14},{18,... | collective-permute-start | bytes 32 | tf_op jit(solution)/shard_map/ppermute | solution.py:12
  212.9 6.9 %collective-permute-start.18 = (bf16[2,512,512]{2,1,0:T(8,128)(2,1)}, bf16[2,512,512]{2,1,0:T(8,128)(2,1)}, u32[]{:S(2)}, u32[]{:S(2)}) collective-permute-start(bf16[2,512,512]{2,1,0:T(8,128)(2,1)} %collective-permute-done.14), channel_id=1, source_target_pairs={{0,30},{2,0},{4,2},{6,4},{8,6},{10,8},{12,10},{14,12},{16,14},{18,... | collective-permute-start | bytes 3145736 | tf_op jit(solution)/shard_map/ppermute | solution.py:12
  219.9 1.9 collective-permute-start.15
  223.8 10.1 %collective-permute-done.28 = s32[2]{0:T(128)S(1)} collective-permute-done((s32[2]{0:T(128)S(1)}, s32[2]{0:T(128)S(1)}, u32[]{:S(2)}, u32[]{:S(2)}) %collective-permute-start.28) | collective-permute-done | bytes 40 | tf_op jit(solution)/shard_map/ppermute | solution.py:12
  239.5 2.1 collective-permute-start.19
  241.7 7.4 %collective-permute-start.22 = (bf16[2,512,512]{2,1,0:T(8,128)(2,1)}, bf16[2,512,512]{2,1,0:T(8,128)(2,1)}, u32[]{:S(2)}, u32[]{:S(2)}) collective-permute-start(bf16[2,512,512]{2,1,0:T(8,128)(2,1)} %collective-permute-done.18), channel_id=1, source_target_pairs={{0,30},{2,0},{4,2},{6,4},{8,6},{10,8},{12,10},{14,12},{16,14},{18,... | collective-permute-start | bytes 3145736 | tf_op jit(solution)/shard_map/ppermute | solution.py:12
  250.1 2.5 collective-permute-done.19
  252.6 3.3 collective-permute-start.23
  258.8 3.5 collective-permute-done.22
  262.3 7.4 %collective-permute-start.26 = (bf16[2,512,512]{2,1,0:T(8,128)(2,1)}, bf16[2,512,512]{2,1,0:T(8,128)(2,1)S(1)}, u32[]{:S(2)}, u32[]{:S(2)}) collective-permute-start(bf16[2,512,512]{2,1,0:T(8,128)(2,1)} %collective-permute-done.22), channel_id=1, source_target_pairs={{0,30},{2,0},{4,2},{6,4},{8,6},{10,8},{12,10},{14,12},{16,14},{18,... | collective-permute-start | bytes 3145736 | tf_op jit(solution)/shard_map/ppermute | solution.py:12
  272.9 2.1 collective-permute-start.27
  278.2 2.5 fusion.21
  280.7 3.2 collective-permute-done.26
  283.9 7.3 %collective-permute-start.30 = (bf16[2,512,512]{2,1,0:T(8,128)(2,1)S(1)}, bf16[2,512,512]{2,1,0:T(8,128)(2,1)S(1)}, u32[]{:S(2)}, u32[]{:S(2)}) collective-permute-start(bf16[2,512,512]{2,1,0:T(8,128)(2,1)S(1)} %collective-permute-done.26), channel_id=1, source_target_pairs={{0,30},{2,0},{4,2},{6,4},{8,6},{10,8},{12,10},{14,12},{16,14},{18,... | collective-permute-start | bytes 3145736 | tf_op jit(solution)/shard_map/ppermute | solution.py:12
  291.2 2.5 fusion.22
  293.8 2.1 collective-permute-start.31
  295.9 2.4 fusion.19
  298.3 2.4 fusion.20
  303.3 6.1 %collective-permute-done.31 = bf16[1024,384]{1,0:T(8,128)(2,1)S(1)} collective-permute-done((bf16[1024,384]{1,0:T(8,128)(2,1)S(1)}, bf16[1024,384]{1,0:T(8,128)(2,1)S(1)}, u32[]{:S(2)}, u32[]{:S(2)}) %collective-permute-start.31) | collective-permute-done | bytes 786464 | tf_op jit(solution)/shard_map/ppermute | solution.py:12
  312.1 6.3 %fusion = f32[1024,384]{1,0:T(8,128)} fusion(f32[512,384]{1,0:T(8,128)} %fusion.15, f32[1024]{0:T(1024)S(1)} %bitcast.292, f32[512,384]{1,0:T(8,128)} %fusion.16, f32[1024]{0:T(1024)S(1)} %bitcast.293, f32[512,384]{1,0:T(8,128)} %fusion.17, f32[1024]{0:T(1024)S(1)} %bitcast.290, f32[512,384]{1,0:T(8,128)} %fusion.18, f32[1024]{0:T(1024)S(1)} %bitcast.291, ...), kind=kLoop, calls=%fused_computation.1 | loop fusion | flops 12189696 | bytes 14221312 | tf_op jit(solution)/shard_map/add | solution.py:26
  318.4 33.2 %reduce-scatter.2.cloned.1.call-done = f32[512,384]{1,0:T(8,128)} async-done(((f32[1024,384]{1,0:T(8,128)}), f32[512,384]{1,0:T(8,128)}) %reduce-scatter.2.cloned.1.call-update) | async-done | bytes 786448 | tf_op jit(solution)/shard_map/reduce_scatter | solution.py:57
  352.8 24.0 %psum.14 = f32[384]{0:T(512)S(1)} all-reduce(f32[384]{0:T(512)S(1)} %multiply_reduce_fusion), channel_id=1, replica_groups=mesh['row'=16,'col'=16,'layer'=2] {'row'}, use_global_device_ids=true, to_apply=%region_2.3 | all-reduce | flops 384 | bytes 3072 | tf_op jit(solution)/shard_map/psum | solution.py:61
  376.8 8.9 %psum.15 = f32[384]{0:T(512)S(1)} all-reduce(f32[384]{0:T(512)S(1)} %psum.14), channel_id=1, replica_groups=mesh['row'=16,'col'=16,'layer'=2] {'layer'}, use_global_device_ids=true, to_apply=%region_3.4 | all-reduce | flops 384 | bytes 3072 | tf_op jit(solution)/shard_map/psum | solution.py:61
  385.7 2.1 multiply_divide_fusion
  (100 shorter events, 31.8 us)
Async XLA Ops:
  6.5 345.0 %reduce-scatter.2.cloned.1.call-start = ((), (), s32[]{:S(2)}) async-start(), calls=%async_computation.1 | async-start | bytes 2359296 | tf_op jit(solution)/shard_map/reduce_scatter | solution.py:57
  6.5 35.0 %collective-permute-start = (s32[2]{0:T(128)}, s32[2]{0:T(128)S(1)}, u32[]{:S(2)}, u32[]{:S(2)}) collective-permute-start(s32[2]{0:T(128)} %bitcast.294), channel_id=1, source_target_pairs={{0,16},{2,18},{4,20},{6,22},{8,24},{10,26},{12,28},{14,30},{16,0},... | collective-permute-start | bytes 32 | tf_op jit(solution)/shard_map/ppermute | solution.py:12
  12.0 22.9 %collective-permute-start.1 = (s32[]{:T(128)}, s32[]{:T(128)}, u32[]{:S(2)}, u32[]{:S(2)}) collective-permute-start(s32[]{:T(128)} %bitcast.2), channel_id=1, source_target_pairs={{0,16},{2,18},{4,20},{6,22},{8,24},{10,26},{12,28},{14,30},{16,0},... | collective-permute-start | bytes 20 | tf_op jit(solution)/shard_map/ppermute | solution.py:12
  13.9 149.4 %collective-permute-start.3 = (bf16[1024,384]{1,0:T(8,128)(2,1)}, bf16[1024,384]{1,0:T(8,128)(2,1)}, u32[]{:S(2)}, u32[]{:S(2)}) collective-permute-start(bf16[1024,384]{1,0:T(8,128)(2,1)} %bitcast.271), channel_id=1, source_target_pairs={{0,256},{32,288},{64,320},{96,352},{128,384},{160,416},{192,448},{... | collective-permute-start | bytes 2359304 | tf_op jit(solution)/shard_map/ppermute | solution.py:12
  29.6 73.3 %collective-permute-start.2 = (bf16[2,512,512]{2,1,0:T(8,128)(2,1)}, bf16[2,512,512]{2,1,0:T(8,128)(2,1)S(1)}, u32[]{:S(2)}, u32[]{:S(2)}) collective-permute-start(bf16[2,512,512]{2,1,0:T(8,128)(2,1)} %bitcast.270), channel_id=1, source_target_pairs={{0,16},{2,18},{4,20},{6,22},{8,24},{10,26},{12,28},{14,30},{16,0},... | collective-permute-start | bytes 3145736 | tf_op jit(solution)/shard_map/ppermute | solution.py:12
  35.6 14.6 %collective-permute-start.5 = (s32[]{:T(128)}, s32[]{:T(128)}, u32[]{:S(2)}, u32[]{:S(2)}) collective-permute-start(s32[]{:T(128)} %select_n.195), channel_id=1, source_target_pairs={{0,30},{2,0},{4,2},{6,4},{8,6},{10,8},{12,10},{14,12},{16,14},{18,... | collective-permute-start | bytes 20 | tf_op jit(solution)/shard_map/ppermute | solution.py:12
  47.7 15.5 %collective-permute-start.4 = (s32[2]{0:T(128)S(1)}, s32[2]{0:T(128)S(1)}, u32[]{:S(2)}, u32[]{:S(2)}) collective-permute-start(s32[2]{0:T(128)S(1)} %broadcast_select_fusion.2), channel_id=1, source_target_pairs={{0,30},{2,0},{4,2},{6,4},{8,6},{10,8},{12,10},{14,12},{16,14},{18,... | collective-permute-start | bytes 32 | tf_op jit(solution)/shard_map/ppermute | solution.py:12
  51.7 4.9 %collective-permute-start.9 = (s32[]{:T(128)}, s32[]{:T(128)}, u32[]{:S(2)}, u32[]{:S(2)}) collective-permute-start(s32[]{:T(128)} %collective-permute-done.5), channel_id=1, source_target_pairs={{0,30},{2,0},{4,2},{6,4},{8,6},{10,8},{12,10},{14,12},{16,14},{18,... | collective-permute-start | bytes 20 | tf_op jit(solution)/shard_map/ppermute | solution.py:12
  57.7 11.4 %collective-permute-start.13 = (s32[]{:T(128)}, s32[]{:T(128)}, u32[]{:S(2)}, u32[]{:S(2)}) collective-permute-start(s32[]{:T(128)} %collective-permute-done.9), channel_id=1, source_target_pairs={{0,30},{2,0},{4,2},{6,4},{8,6},{10,8},{12,10},{14,12},{16,14},{18,... | collective-permute-start | bytes 20 | tf_op jit(solution)/shard_map/ppermute | solution.py:12
  70.6 26.5 %collective-permute-start.8 = (s32[2]{0:T(128)S(1)}, s32[2]{0:T(128)S(1)}, u32[]{:S(2)}, u32[]{:S(2)}) collective-permute-start(s32[2]{0:T(128)S(1)} %collective-permute-done.4), channel_id=1, source_target_pairs={{0,30},{2,0},{4,2},{6,4},{8,6},{10,8},{12,10},{14,12},{16,14},{18,... | collective-permute-start | bytes 32 | tf_op jit(solution)/shard_map/ppermute | solution.py:12
  84.6 4.5 %collective-permute-start.17 = (s32[]{:T(128)}, s32[]{:T(128)}, u32[]{:S(2)}, u32[]{:S(2)}) collective-permute-start(s32[]{:T(128)} %collective-permute-done.13), channel_id=1, source_target_pairs={{0,30},{2,0},{4,2},{6,4},{8,6},{10,8},{12,10},{14,12},{16,14},{18,... | collective-permute-start | bytes 20 | tf_op jit(solution)/shard_map/ppermute | solution.py:12
  90.2 18.1 %collective-permute-start.21 = (s32[]{:T(128)}, s32[]{:T(128)}, u32[]{:S(2)}, u32[]{:S(2)}) collective-permute-start(s32[]{:T(128)} %collective-permute-done.17), channel_id=1, source_target_pairs={{0,30},{2,0},{4,2},{6,4},{8,6},{10,8},{12,10},{14,12},{16,14},{18,... | collective-permute-start | bytes 20 | tf_op jit(solution)/shard_map/ppermute | solution.py:12
  104.3 33.7 %collective-permute-start.6 = (bf16[2,512,512]{2,1,0:T(8,128)(2,1)S(1)}, bf16[2,512,512]{2,1,0:T(8,128)(2,1)S(1)}, u32[]{:S(2)}, u32[]{:S(2)}) collective-permute-start(bf16[2,512,512]{2,1,0:T(8,128)(2,1)S(1)} %broadcast_select_fusion), channel_id=1, source_target_pairs={{0,30},{2,0},{4,2},{6,4},{8,6},{10,8},{12,10},{14,12},{16,14},{18,... | collective-permute-start | bytes 3145736 | tf_op jit(solution)/shard_map/ppermute | solution.py:12
  106.4 25.4 %collective-permute-start.12 = (s32[2]{0:T(128)S(1)}, s32[2]{0:T(128)S(1)}, u32[]{:S(2)}, u32[]{:S(2)}) collective-permute-start(s32[2]{0:T(128)S(1)} %collective-permute-done.8), channel_id=1, source_target_pairs={{0,30},{2,0},{4,2},{6,4},{8,6},{10,8},{12,10},{14,12},{16,14},{18,... | collective-permute-start | bytes 32 | tf_op jit(solution)/shard_map/ppermute | solution.py:12
  109.7 15.4 %collective-permute-start.25 = (s32[]{:T(128)}, s32[]{:T(128)}, u32[]{:S(2)}, u32[]{:S(2)}) collective-permute-start(s32[]{:T(128)} %collective-permute-done.21), channel_id=1, source_target_pairs={{0,30},{2,0},{4,2},{6,4},{8,6},{10,8},{12,10},{14,12},{16,14},{18,... | collective-permute-start | bytes 20 | tf_op jit(solution)/shard_map/ppermute | solution.py:12
  126.2 13.7 %collective-permute-start.29 = (s32[]{:T(128)}, s32[]{:T(128)}, u32[]{:S(2)}, u32[]{:S(2)}) collective-permute-start(s32[]{:T(128)} %collective-permute-done.25), channel_id=1, source_target_pairs={{0,30},{2,0},{4,2},{6,4},{8,6},{10,8},{12,10},{14,12},{16,14},{18,... | collective-permute-start | bytes 20 | tf_op jit(solution)/shard_map/ppermute | solution.py:12
  137.9 31.3 %collective-permute-start.10 = (bf16[2,512,512]{2,1,0:T(8,128)(2,1)S(1)}, bf16[2,512,512]{2,1,0:T(8,128)(2,1)}, u32[]{:S(2)}, u32[]{:S(2)}) collective-permute-start(bf16[2,512,512]{2,1,0:T(8,128)(2,1)S(1)} %collective-permute-done.6), channel_id=1, source_target_pairs={{0,30},{2,0},{4,2},{6,4},{8,6},{10,8},{12,10},{14,12},{16,14},{18,... | collective-permute-start | bytes 3145736 | tf_op jit(solution)/shard_map/ppermute | solution.py:12
  141.2 16.6 %collective-permute-start.16 = (s32[2]{0:T(128)S(1)}, s32[2]{0:T(128)S(1)}, u32[]{:S(2)}, u32[]{:S(2)}) collective-permute-start(s32[2]{0:T(128)S(1)} %collective-permute-done.12), channel_id=1, source_target_pairs={{0,30},{2,0},{4,2},{6,4},{8,6},{10,8},{12,10},{14,12},{16,14},{18,... | collective-permute-start | bytes 32 | tf_op jit(solution)/shard_map/ppermute | solution.py:12
  164.8 32.0 %collective-permute-start.7 = (bf16[1024,384]{1,0:T(8,128)(2,1)S(1)}, bf16[1024,384]{1,0:T(8,128)(2,1)}, u32[]{:S(2)}, u32[]{:S(2)}) collective-permute-start(bf16[1024,384]{1,0:T(8,128)(2,1)S(1)} %broadcast_select_fusion.1), channel_id=1, source_target_pairs={{0,480},{32,0},{64,32},{96,64},{128,96},{160,128},{192,160},{224,1... | collective-permute-start | bytes 2359304 | tf_op jit(solution)/shard_map/ppermute | solution.py:12
  169.3 43.6 %collective-permute-start.14 = (bf16[2,512,512]{2,1,0:T(8,128)(2,1)}, bf16[2,512,512]{2,1,0:T(8,128)(2,1)}, u32[]{:S(2)}, u32[]{:S(2)}) collective-permute-start(bf16[2,512,512]{2,1,0:T(8,128)(2,1)} %collective-permute-done.10), channel_id=1, source_target_pairs={{0,30},{2,0},{4,2},{6,4},{8,6},{10,8},{12,10},{14,12},{16,14},{18,... | collective-permute-start | bytes 3145736 | tf_op jit(solution)/shard_map/ppermute | solution.py:12
  174.9 16.2 %collective-permute-start.20 = (s32[2]{0:T(128)S(1)}, s32[2]{0:T(128)S(1)}, u32[]{:S(2)}, u32[]{:S(2)}) collective-permute-start(s32[2]{0:T(128)S(1)} %collective-permute-done.16), channel_id=1, source_target_pairs={{0,30},{2,0},{4,2},{6,4},{8,6},{10,8},{12,10},{14,12},{16,14},{18,... | collective-permute-start | bytes 32 | tf_op jit(solution)/shard_map/ppermute | solution.py:12
  196.8 23.1 %collective-permute-start.11 = (bf16[1024,384]{1,0:T(8,128)(2,1)}, bf16[1024,384]{1,0:T(8,128)(2,1)}, u32[]{:S(2)}, u32[]{:S(2)}) collective-permute-start(bf16[1024,384]{1,0:T(8,128)(2,1)} %collective-permute-done.7), channel_id=1, source_target_pairs={{0,480},{32,0},{64,32},{96,64},{128,96},{160,128},{192,160},{224,1... | collective-permute-start | bytes 2359304 | tf_op jit(solution)/shard_map/ppermute | solution.py:12
  199.0 8.1 %collective-permute-start.24 = (s32[2]{0:T(128)S(1)}, s32[2]{0:T(128)S(1)}, u32[]{:S(2)}, u32[]{:S(2)}) collective-permute-start(s32[2]{0:T(128)S(1)} %collective-permute-done.20), channel_id=1, source_target_pairs={{0,30},{2,0},{4,2},{6,4},{8,6},{10,8},{12,10},{14,12},{16,14},{18,... | collective-permute-start | bytes 32 | tf_op jit(solution)/shard_map/ppermute | solution.py:12
  212.9 28.8 %collective-permute-start.18 = (bf16[2,512,512]{2,1,0:T(8,128)(2,1)}, bf16[2,512,512]{2,1,0:T(8,128)(2,1)}, u32[]{:S(2)}, u32[]{:S(2)}) collective-permute-start(bf16[2,512,512]{2,1,0:T(8,128)(2,1)} %collective-permute-done.14), channel_id=1, source_target_pairs={{0,30},{2,0},{4,2},{6,4},{8,6},{10,8},{12,10},{14,12},{16,14},{18,... | collective-permute-start | bytes 3145736 | tf_op jit(solution)/shard_map/ppermute | solution.py:12
  219.9 19.7 %collective-permute-start.15 = (bf16[1024,384]{1,0:T(8,128)(2,1)}, bf16[1024,384]{1,0:T(8,128)(2,1)}, u32[]{:S(2)}, u32[]{:S(2)}) collective-permute-start(bf16[1024,384]{1,0:T(8,128)(2,1)} %collective-permute-done.11), channel_id=1, source_target_pairs={{0,480},{32,0},{64,32},{96,64},{128,96},{160,128},{192,160},{224,1... | collective-permute-start | bytes 2359304 | tf_op jit(solution)/shard_map/ppermute | solution.py:12
  221.9 12.1 %collective-permute-start.28 = (s32[2]{0:T(128)S(1)}, s32[2]{0:T(128)S(1)}, u32[]{:S(2)}, u32[]{:S(2)}) collective-permute-start(s32[2]{0:T(128)S(1)} %collective-permute-done.24), channel_id=1, source_target_pairs={{0,30},{2,0},{4,2},{6,4},{8,6},{10,8},{12,10},{14,12},{16,14},{18,... | collective-permute-start | bytes 32 | tf_op jit(solution)/shard_map/ppermute | solution.py:12
  239.5 13.0 %collective-permute-start.19 = (bf16[1024,384]{1,0:T(8,128)(2,1)}, bf16[1024,384]{1,0:T(8,128)(2,1)}, u32[]{:S(2)}, u32[]{:S(2)}) collective-permute-start(bf16[1024,384]{1,0:T(8,128)(2,1)} %collective-permute-done.15), channel_id=1, source_target_pairs={{0,480},{32,0},{64,32},{96,64},{128,96},{160,128},{192,160},{224,1... | collective-permute-start | bytes 2359304 | tf_op jit(solution)/shard_map/ppermute | solution.py:12
  241.7 20.6 %collective-permute-start.22 = (bf16[2,512,512]{2,1,0:T(8,128)(2,1)}, bf16[2,512,512]{2,1,0:T(8,128)(2,1)}, u32[]{:S(2)}, u32[]{:S(2)}) collective-permute-start(bf16[2,512,512]{2,1,0:T(8,128)(2,1)} %collective-permute-done.18), channel_id=1, source_target_pairs={{0,30},{2,0},{4,2},{6,4},{8,6},{10,8},{12,10},{14,12},{16,14},{18,... | collective-permute-start | bytes 3145736 | tf_op jit(solution)/shard_map/ppermute | solution.py:12
  252.6 20.4 %collective-permute-start.23 = (bf16[1024,384]{1,0:T(8,128)(2,1)}, bf16[1024,384]{1,0:T(8,128)(2,1)S(1)}, u32[]{:S(2)}, u32[]{:S(2)}) collective-permute-start(bf16[1024,384]{1,0:T(8,128)(2,1)} %collective-permute-done.19), channel_id=1, source_target_pairs={{0,480},{32,0},{64,32},{96,64},{128,96},{160,128},{192,160},{224,1... | collective-permute-start | bytes 2359304 | tf_op jit(solution)/shard_map/ppermute | solution.py:12
  262.3 21.6 %collective-permute-start.26 = (bf16[2,512,512]{2,1,0:T(8,128)(2,1)}, bf16[2,512,512]{2,1,0:T(8,128)(2,1)S(1)}, u32[]{:S(2)}, u32[]{:S(2)}) collective-permute-start(bf16[2,512,512]{2,1,0:T(8,128)(2,1)} %collective-permute-done.22), channel_id=1, source_target_pairs={{0,30},{2,0},{4,2},{6,4},{8,6},{10,8},{12,10},{14,12},{16,14},{18,... | collective-permute-start | bytes 3145736 | tf_op jit(solution)/shard_map/ppermute | solution.py:12
  272.9 20.8 %collective-permute-start.27 = (bf16[1024,384]{1,0:T(8,128)(2,1)S(1)}, bf16[1024,384]{1,0:T(8,128)(2,1)S(1)}, u32[]{:S(2)}, u32[]{:S(2)}) collective-permute-start(bf16[1024,384]{1,0:T(8,128)(2,1)S(1)} %collective-permute-done.23), channel_id=1, source_target_pairs={{0,480},{32,0},{64,32},{96,64},{128,96},{160,128},{192,160},{224,1... | collective-permute-start | bytes 2359304 | tf_op jit(solution)/shard_map/ppermute | solution.py:12
  283.9 25.5 %collective-permute-start.30 = (bf16[2,512,512]{2,1,0:T(8,128)(2,1)S(1)}, bf16[2,512,512]{2,1,0:T(8,128)(2,1)S(1)}, u32[]{:S(2)}, u32[]{:S(2)}) collective-permute-start(bf16[2,512,512]{2,1,0:T(8,128)(2,1)S(1)} %collective-permute-done.26), channel_id=1, source_target_pairs={{0,30},{2,0},{4,2},{6,4},{8,6},{10,8},{12,10},{14,12},{16,14},{18,... | collective-permute-start | bytes 3145736 | tf_op jit(solution)/shard_map/ppermute | solution.py:12
  293.8 15.6 %collective-permute-start.31 = (bf16[1024,384]{1,0:T(8,128)(2,1)S(1)}, bf16[1024,384]{1,0:T(8,128)(2,1)S(1)}, u32[]{:S(2)}, u32[]{:S(2)}) collective-permute-start(bf16[1024,384]{1,0:T(8,128)(2,1)S(1)} %collective-permute-done.27), channel_id=1, source_target_pairs={{0,480},{32,0},{64,32},{96,64},{128,96},{160,128},{192,160},{224,1... | collective-permute-start | bytes 2359304 | tf_op jit(solution)/shard_map/ppermute | solution.py:12
Sparse Core Ops, SparseCore 0:
  318.5 32.9 reduce-scatter.1
